TPU v7x, 128 devices: a whole 4x4x4 slice. The times are simulated.
128 devices in a mesh: row: 8 (over y, z_lo), col: 16 (over x, z_hi, core).
Axes of the slice: x: 4, y: 4, z: 4 (z_hi: 2, z_lo: 2; z = z_hi * 2 + z_lo), core: 2. Of those that a mesh axis runs over, the one named last changes fastest.
Arguments:
- tokens: bfloat16 [1024, 53248], P(('row', 'col')), may hold values from -6 to 6
- eigvecs: float32 [53248, 2048], P('row', 'col'), may hold values from -0.02734375 to 0.02734375
- eigvals: float32 [2048], P('col'), may hold values from 0.25 to 4
- v_first: float32 [53248, 256], P(('row', 'col')), may hold values from -0.109375 to 0.109375
- v_second: float32 [53248, 256], P(('row', 'col')), may hold values from -0.109375 to 0.109375
- t_first: float32 [256, 256], replicated, may hold values from -0.375 to 0.375
- t_second: float32 [256, 256], replicated, may hold values from -0.375 to 0.375
Outputs:
- whitened: float32 [1024, 2048], P('row', 'col')
All inputs are finite; a program needn't handle non-finite values.
Results may differ from a plain program's by a relative error of at most 0.0029.
Values may be sent and summed in bfloat16 or wider, within the bound.
A program may use at most 128 MiB of HBM per device.

v0:
```python
import jax
import jax.numpy as jnp
from jax import lax
from jax.sharding import PartitionSpec as P


def local_update(block, panel, factor, inner):
    middle = jnp.dot(
        factor, inner, precision=lax.Precision.HIGHEST, preferred_element_type=jnp.float32
    )
    return block - jnp.dot(
        panel, middle, precision=lax.Precision.HIGHEST, preferred_element_type=jnp.float32
    )


def partial_inner(panel, block):
    return jnp.dot(
        panel.T, block, precision=lax.Precision.HIGHEST, preferred_element_type=jnp.float32
    )


def per_device(tokens, eigvecs, eigvals, v_first, v_second, t_first, t_second):
    panels = (
        lax.all_gather(v_first, "col", axis=0, tiled=True),
        lax.all_gather(v_second, "col", axis=0, tiled=True),
    )
    block = eigvecs
    for panel, factor in ((panels[1], t_second), (panels[0], t_first)):
        inner = lax.psum(partial_inner(panel, block), "row")
        block = local_update(block, panel, factor, inner)
    whitening = (block * lax.rsqrt(eigvals)[None, :]).astype(jnp.bfloat16)
    row_tokens = lax.all_gather(tokens, "col", axis=0, tiled=True)
    slab = lax.all_to_all(row_tokens, "row", split_axis=1, concat_axis=0, tiled=True)
    partial_value = jnp.dot(slab, whitening, preferred_element_type=jnp.float32)
    summed = lax.psum_scatter(partial_value, "row", scatter_dimension=0, tiled=True)
    return summed


def solution(mesh):
    in_specs = (
        P(("row", "col"), None),
        P("row", "col"),
        P("col"),
        P(("row", "col"), None),
        P(("row", "col"), None),
        P(),
        P(),
    )
    out_specs = P("row", "col")
    return jax.shard_map(
        per_device, mesh=mesh, in_specs=in_specs, out_specs=out_specs, check_vma=False
    )
```

profile of v0, /device:TPU:1, one launch (start us, length us, event | category | flops | bytes accessed | tf_op | source)
XLA Modules:
  0.0 649.0 jit_solution(17153606568712980208)
XLA Ops:
  6.5 0.0 copy-start
  6.5 0.0 all-gather.4.cloned.1.call-start
  6.5 0.7 all-gather.4.cloned.1.call-update
  7.3 0.0 all-gather.8.cloned.1.call-start
  7.3 0.7 all-gather.8.cloned.1.call-update
  8.0 0.0 all-reduce.3.cloned.1.call-start
  8.1 71.8 %all-gather.4.cloned.1.call-done = f32[6656,256]{1,0:T(8,128)} async-done(((f32[416,256]{1,0:T(8,128)}), f32[6656,256]{1,0:T(8,128)}) %all-gather.4.cloned.1.call-update) | async-done | bytes 6815760 | tf_op jit(solution)/shard_map/all_gather | solution.py:25
  79.9 14.6 %fusion.4 = f32[256,128]{1,0:T(8,128)} fusion(f32[6656,256]{1,0:T(8,128)} %all-gather.4.cloned.1.call-done, f32[6656,128]{1,0:T(8,128)} %param.8), kind=kOutput, calls=%fused_computation.8 | convolution fusion | flops 2617245696 | bytes 10354688 | tf_op jit(solution)/shard_map/dot_general | solution.py:17
  94.5 0.0 all-reduce.3.cloned.1.call-update
  94.5 0.0 all-gather.6.cloned.1.call-start
  94.6 0.5 all-gather.6.cloned.1.call-update
  95.1 80.9 %all-gather.8.cloned.1.call-done = bf16[128,53248]{1,0:T(8,128)(2,1)} async-done(((bf16[8,53248]{1,0:T(8,128)(2,1)}), bf16[128,53248]{1,0:T(8,128)(2,1)}) %all-gather.8.cloned.1.call-update) | async-done | bytes 13631504 | tf_op jit(solution)/shard_map/all_gather | solution.py:32
  176.0 18.4 %copy.17 = bf16[128,53248]{0,1:T(8,128)(2,1)} copy(bf16[128,53248]{1,0:T(8,128)(2,1)} %all-gather.8.cloned.1.call-done) | data formatting | bytes 27262976 | tf_op jit(solution)/shard_map/all_gather | solution.py:32
  194.4 5.4 all-to-all-start
  199.9 0.2 all-reduce.5.cloned.1.call-start
  200.1 5.1 copy.16
  205.2 210.6 %all-reduce.3.cloned.1.call-done = f32[256,128]{1,0:T(8,128)} async-done(((f32[256,128]{1,0:T(8,128)}), f32[256,128]{1,0:T(8,128)}) %all-reduce.3.cloned.1.call-update) | async-done | bytes 131088 | tf_op jit(solution)/shard_map/psum | solution.py:29
  415.8 0.0 copy-done
  415.8 1.3 fusion.5
  417.1 12.6 %fusion.2 = f32[6656,128]{0,1:T(8,128)} fusion(f32[6656,128]{0,1:T(8,128)} %copy.16, f32[128,256]{1,0:T(8,128)S(1)} %fusion.5, f32[6656,256]{1,0:T(8,128)} %all-gather.4.cloned.1.call-done), kind=kOutput, calls=%fused_computation.4 | convolution fusion | flops 2618097664 | bytes 13762560 | tf_op jit(solution)/shard_map/dot_general | solution.py:11
  429.7 0.0 copy-start.3
  429.7 0.0 copy-start.2
  429.7 60.0 %all-gather.6.cloned.1.call-done = f32[6656,256]{1,0:T(8,128)} async-done(((f32[416,256]{1,0:T(8,128)}), f32[6656,256]{1,0:T(8,128)}) %all-gather.6.cloned.1.call-update) | async-done | bytes 6815760 | tf_op jit(solution)/shard_map/all_gather | solution.py:24
  489.7 7.9 %convolution_bitcast_fusion.3 = f32[256,128]{0,1:T(8,128)} fusion(f32[6656,128]{0,1:T(8,128)} %fusion.2, f32[6656,256]{1,0:T(8,128)} %all-gather.6.cloned.1.call-done), kind=kOutput, calls=%fused_computation.7 | convolution fusion | flops 2617245696 | bytes 10354688 | tf_op jit(solution)/shard_map/dot_general | solution.py:17
  497.6 0.0 all-reduce.5.cloned.1.call-update
  497.7 0.3 reduce-scatter.2.cloned.1.call-start
  497.9 0.0 copy-done.3
  498.0 65.3 %all-reduce.5.cloned.1.call-done = f32[256,128]{0,1:T(8,128)} async-done(((f32[256,128]{0,1:T(8,128)}), f32[256,128]{0,1:T(8,128)}) %all-reduce.5.cloned.1.call-update) | async-done | bytes 131088 | tf_op jit(solution)/shard_map/psum | solution.py:29
  563.3 0.0 copy-done.2
  563.3 1.3 fusion.6
  564.6 10.8 %fusion.3 = bf16[6656,128]{0,1:T(8,128)(2,1)S(1)} fusion(f32[6656,128]{0,1:T(8,128)} %fusion.2, f32[128,256]{1,0:T(8,128)S(1)} %fusion.6, f32[6656,256]{1,0:T(8,128)} %all-gather.6.cloned.1.call-done, f32[128]{0:T(128)S(1)} %rsqrt.3), kind=kOutput, calls=%fused_computation.5 | convolution fusion | flops 2619801600 | bytes 12059136 | tf_op jit(solution)/shard_map/dot_general | solution.py:11
  575.4 0.0 all-to-all-done
  575.4 17.6 %copy.18 = bf16[8,128,6656]{2,1,0:T(8,128)(2,1)} copy(bf16[8,128,6656]{1,2,0:T(8,128)(2,1)} %bitcast.4) | data formatting | bytes 27262976 | tf_op jit(solution)/shard_map/all_to_all | solution.py:33
  593.0 0.0 copy-start.1
  593.0 10.1 %convolution_bitcast_fusion.2 = f32[1024,128]{0,1:T(8,128)} fusion(bf16[6656,128]{0,1:T(8,128)(2,1)S(1)} %fusion.3, bf16[1024,6656]{1,0:T(8,128)(2,1)} %bitcast.34), kind=kOutput, calls=%fused_computation.6 | convolution fusion | flops 1744830464 | bytes 15859712 | tf_op jit(solution)/shard_map/dot_general | solution.py:34
  603.1 0.0 reduce-scatter.2.cloned.1.call-update
  603.1 37.5 %reduce-scatter.2.cloned.1.call-done = f32[128,128]{0,1:T(8,128)} async-done(((f32[1024,128]{0,1:T(8,128)}), f32[128,128]{0,1:T(8,128)}) %reduce-scatter.2.cloned.1.call-update) | async-done | bytes 65552 | tf_op jit(solution)/shard_map/reduce_scatter | solution.py:35
  640.6 1.6 copy.19
  642.2 0.0 copy-done.1
  (1 shorter events, 0.0 us)
Async XLA Ops:
  6.5 409.3 %copy-start = (f32[256,256]{1,0:T(8,128)S(1)}, f32[256,256]{1,0:T(8,128)}, u32[]{:S(2)}) copy-start(f32[256,256]{1,0:T(8,128)} %param.13) | copy-start | bytes 786436
  6.5 73.3 %all-gather.4.cloned.1.call-start = ((), (), s32[]{:S(2)}) async-start(), calls=%async_computation.2 | async-start | bytes 7241728 | tf_op jit(solution)/shard_map/all_gather | solution.py:25
  7.3 168.7 %all-gather.8.cloned.1.call-start = ((), (), s32[]{:S(2)}) async-start(), calls=%async_computation.6 | async-start | bytes 14483456 | tf_op jit(solution)/shard_map/all_gather | solution.py:32
  8.0 407.8 %all-reduce.3.cloned.1.call-start = ((), (), s32[]{:S(2)}) async-start(), calls=%async_computation.3 | async-start | bytes 262144 | tf_op jit(solution)/shard_map/psum | solution.py:29
  94.5 395.2 %all-gather.6.cloned.1.call-start = ((), (), s32[]{:S(2)}) async-start(), calls=%async_computation.4 | async-start | bytes 7241728 | tf_op jit(solution)/shard_map/all_gather | solution.py:24
  194.4 381.0 %all-to-all-start = ((bf16[128,8,6656]{0,2,1:T(8,128)(2,1)}), bf16[128,8,6656]{0,2,1:T(8,128)(2,1)}, u32[]{:S(2)}, u32[]{:S(2)}) async-start(bf16[128,8,6656]{0,2,1:T(8,128)(2,1)} %bitcast.33), calls=%async_computation | async-start | bytes 27262976 | tf_op jit(solution)/shard_map/all_to_all | solution.py:33
  199.9 363.4 %all-reduce.5.cloned.1.call-start = ((), (), s32[]{:S(2)}) async-start(), calls=%async_computation.5 | async-start | bytes 262144 | tf_op jit(solution)/shard_map/psum | solution.py:29
  429.7 68.2 %copy-start.3 = (f32[128]{0:T(128)S(1)}, f32[128]{0:T(128)}, u32[]{:S(2)}) copy-start(f32[128]{0:T(128)} %param.9) | copy-start | bytes 1540
  429.7 133.6 %copy-start.2 = (f32[256,256]{1,0:T(8,128)S(1)}, f32[256,256]{1,0:T(8,128)}, u32[]{:S(2)}) copy-start(f32[256,256]{1,0:T(8,128)} %param.12) | copy-start | bytes 786436
  497.7 143.0 %reduce-scatter.2.cloned.1.call-start = ((), (), s32[]{:S(2)}) async-start(), calls=%async_computation.7 | async-start | bytes 589824 | tf_op jit(solution)/shard_map/reduce_scatter | solution.py:35
  593.0 49.2 %copy-start.1 = (f32[256,256]{1,0:T(8,128)S(1)}, f32[256,256]{1,0:T(8,128)}, u32[]{:S(2)}) copy-start(f32[256,256]{1,0:T(8,128)} %param.13) | copy-start | bytes 786436
Sparse Core Ops, SparseCore 0:
  9.8 70.0 all-gather.3
  82.3 93.6 all-gather.7
  178.5 237.2 all-reduce.2
  418.3 71.3 all-gather.5
  497.8 65.4 all-reduce.4
  603.2 37.3 reduce-scatter.1
where the time goes:
time: 655 us; the launch traced here: 649 us
  waiting for transfers between devices  528 us (81%)
  matrix products  58.7 us (9%)
  local copies, waits for them, and re-layouts  42.7 us (7%)
  between operations  13.5 us (2%)
    psum x2, waiting for transfers between devices, per_device(): inner = lax.psum(partial_inner(panel, block), 'row')  276 us
    all_gather x1, waiting for transfers between devices, per_device(): row_tokens = lax.all_gather(tokens, 'col', axis=0, tiled=True)  80.9 us
    all_gather x1, waiting for transfers between devices, per_device(): lax.all_gather(v_second, 'col', axis=0, tiled=True)  71.8 us
    all_gather x1, waiting for transfers between devices, per_device(): lax.all_gather(v_first, 'col', axis=0, tiled=True)  60 us
    reduce_scatter x1, waiting for transfers between devices, per_device(): lax.psum_scatter(partial_value, 'row', scatter_dimension=0, tiled=True)  37.5 us
    dot_general x2, matrix products, local_update(): jnp.dot(panel, middle, precision=lax.Precision.HIGHEST, preferred_element...  23.4 us
    dot_general x2, matrix products, partial_inner(): jnp.dot(panel.T, block, precision=lax.Precision.HIGHEST, preferred_elemen...  22.6 us
    all_gather x1, local copies, waits for them, and re-layouts, per_device(): row_tokens = lax.all_gather(tokens, 'col', axis=0, tiled=True)  18.4 us
  transfers between devices with their start and end apart: 7, of which 6 were waited for; matrix products, arithmetic and copies ran while one was open for 11% of the time, Pallas kernels for 0%

commit v1 on v0

v1 whole, which is shorter than its diff:
```python
import functools

import jax
import jax.numpy as jnp
from jax import lax
from jax.experimental import pallas as pl
from jax.experimental.pallas import tpu as pltpu
from jax.sharding import PartitionSpec as P

MESH = pl.DeviceIdType.MESH
BF16 = jnp.bfloat16
F32 = jnp.float32
HIGH = lax.Precision.HIGHEST

ROWS = 1664
OWN = 416
SLAB = 6656
YSEG = 2 * SLAB
COPIES = 96


def mm(a, b):
    return jnp.dot(a, b, preferred_element_type=F32)


def exact(a, b):
    return jnp.dot(a, b, precision=HIGH, preferred_element_type=F32)


def kernel(
    x_ref, e_ref, v1_ref, v2_ref, t1_ref, t2_ref, ev_ref, out_ref,
    xy, xs, xb, x2, es, eb, vb, vt, vq, vc,
    p, ry, s, rz, s2, rx, xv,
    pv, rv, sv, rvz, sv2, rvx, u, g,
    send, recv, local,
):
    r, c = lax.axis_index("row"), lax.axis_index("col")
    y, zlo = r // 2, r % 2
    x, q = c // 4, c % 4
    zhi, k = q // 2, q % 2

    def at_y(d):
        return (((y + d) % 4) * 2 + zlo, c)

    def at_x(d):
        return (r, ((x + d) % 4) * 4 + q)

    z_far = (r, x * 4 + (1 - zhi) * 2 + k)
    z_near = (y * 2 + 1 - zlo, c)
    z_other = (y * 2 + 1 - zlo, x * 4 + (1 - zhi) * 2 + k)
    sibling = (r, x * 4 + zhi * 2 + 1 - k)

    peers = [at_y(1), at_y(2), at_y(3), at_x(1), at_x(2), at_x(3)]
    peers += [z_far, z_near, z_other, sibling]
    barrier = pltpu.get_barrier_semaphore()
    for peer in peers:
        pl.semaphore_signal(barrier, inc=1, device_id=peer, device_id_type=MESH)

    started = []

    def put(src, dst, device):
        slot = len(started)
        copy = pltpu.make_async_remote_copy(
            src_ref=src, dst_ref=dst, send_sem=send.at[slot], recv_sem=recv.at[slot],
            device_id=device, device_id_type=MESH,
        )
        copy.start()
        started.append(copy)
        return copy

    here = []

    def move(src, dst):
        copy = pltpu.make_async_copy(src, dst, local.at[len(here)])
        copy.start()
        here.append(copy)
        return copy

    for chunk in range(4):
        panel = v2_ref if chunk < 2 else v1_ref
        value = panel[:, (chunk % 2) * 128 : (chunk % 2 + 1) * 128]
        high = value.astype(BF16)
        vb[0, chunk, q] = high
        vb[1, chunk, q] = (value - high.astype(F32)).astype(BF16)

    def cast(i, carry):
        at = pl.ds(pl.multiple_of(i * 208, 208), 208)
        es[at] = e_ref[at].astype(BF16)
        return carry

    lax.fori_loop(0, 32, cast, 0)

    pl.semaphore_wait(barrier, len(peers))

    y_in = {}
    for d in (2, 1, 3):
        to = (y + d) % 4
        src = x_ref.at[:, pl.ds(pl.multiple_of(to * YSEG, 128), YSEG)]
        y_in[d] = put(src, xy.at[d - 1], at_y(d))
    v_far = put(vb.at[:, :, q], vb.at[:, :, q], z_far)
    v_sib = put(vb.at[:, :, q], vb.at[:, :, q], sibling)
    own_cols = pl.ds(pl.multiple_of(x * 128, 128), 128)
    e_in = []
    for e in (2, 1, 3):
        to = (x + e) % 4
        src = es.at[pl.ds(pl.multiple_of(to * ROWS, ROWS), ROWS)]
        e_in.append(put(src, eb.at[:, own_cols], at_x(e)))
    e_own = move(es.at[pl.ds(pl.multiple_of(x * ROWS, ROWS), ROWS)], eb.at[:, own_cols])

    def x_stage(d):
        def piece(zl, to):
            at = zl * SLAB + to * ROWS
            if d == 0:
                return x_ref.at[:, pl.ds(pl.multiple_of(y * YSEG + at, 128), ROWS)]
            return xy.at[d - 1, :, pl.ds(pl.multiple_of(at, 128), ROWS)]

        mine, other = xb.at[d, zlo, x, zhi, k], xs.at[d, x]
        waits = []
        for e in (2, 1, 3):
            to = (x + e) % 4
            waits.append(put(piece(zlo, to), mine, at_x(e)))
            waits.append(put(piece(1 - zlo, to), other, at_x(e)))
        return waits, [move(piece(zlo, x), mine), move(piece(1 - zlo, x), other)]

    def z_stage(d):
        block = xb.at[d, zlo, :, zhi, k]
        return [
            put(block, block, z_far),
            put(xs.at[d], block, z_near),
            put(xs.at[d], block, z_other),
        ]

    x_in, z_in, c_in = {}, {}, {}
    x_in[0] = x_stage(0)
    for d in (2, 1, 3):
        y_in[d].wait_recv()
        x_in[d] = x_stage(d)
    order = (2, 1, 3, 0)
    for d in order:
        for copy in x_in[d][0]:
            copy.wait_recv()
        for copy in x_in[d][1]:
            copy.wait()
        z_in[d] = z_stage(d)

    v_far.wait_recv()
    far = (1 - zhi) * 2 + k
    v_pass = put(vb.at[:, :, far], vb.at[:, :, far], sibling)
    v_sib.wait_recv()
    e_own.wait()
    for copy in e_in:
        copy.wait_recv()
    v_pass.wait_recv()

    for term in range(2):
        vq[:, term * 128 : (term + 1) * 128] = vb[term, q].reshape(ROWS, 128)
        vc[:, term * 128 : (term + 1) * 128] = vb[term, k].reshape(ROWS, 128)
        for chunk in range(4):
            vt[term, chunk * 128 : (chunk + 1) * 128, :] = vb[term, chunk].reshape(ROWS, 128).T
    for half in range(2):
        cols = eb[:, half * 256 : (half + 1) * 256]
        part = mm(vt[0], cols) + mm(vt[1], cols)
        pv[2 * half] = part[:, :128]
        pv[2 * half + 1] = part[:, 128:]
    both = mm(vt[0], vc[...])
    pv[4] = both[:, :128] + both[:, 128:] + mm(vt[1], vc[:, :128])

    v_in = {}
    for d in (2, 1, 3):
        to = (y - d) % 4
        rows = pl.ds(pl.multiple_of(to * 128, 128), 128)
        v_in[d] = put(pv.at[:, rows, :], rv.at[d - 1], at_y(-d))

    for d in order:
        for copy in z_in[d]:
            copy.wait_recv()
        block = xb.at[d, :, :, :, k]
        c_in[d] = put(block, block, sibling)

    def project(d):
        c_in[d].wait_recv()

        def pack(i, carry):
            rows = xb[d, i // 4, i % 4].astype(F32).reshape(32, ROWS)
            x2[pl.ds(pl.multiple_of(i * 32, 32), 32)] = rows.astype(BF16)
            return carry

        lax.fori_loop(0, 8, pack, 0)
        part = mm(x2[...], eb[...])
        for j in range(4):
            p[d, j] = part[:, j * 128 : (j + 1) * 128]
        both = mm(x2[...], vq[...])
        p[d, 4] = both[:, :128] + both[:, 128:]
        if d > 0:
            return put(p.at[d], ry.at[d - 1], at_y(-d))

    p_in = {}
    p_in[2] = project(2)
    p_in[1] = project(1)
    p_in[3] = project(3)

    for d in (1, 3, 2):
        v_in[d].wait_recv()
    own_rows = pl.ds(pl.multiple_of(y * 128, 128), 128)
    sv[...] = pv[:, own_rows, :] + rv[0] + rv[1] + rv[2]
    vz_in = put(sv.at[:, pl.ds(pl.multiple_of((1 - zlo) * 64, 64), 64), :], rvz, z_near)

    project(0)

    vz_in.wait_recv()
    sv2[...] = sv[:, pl.ds(pl.multiple_of(zlo * 64, 64), 64), :] + rvz[...]
    vx_in = []
    for e in (2, 1, 3):
        vx_in.append(put(sv2.at[(x + e) % 4], rvx.at[e - 1, 0], at_x(e)))
        vx_in.append(put(sv2.at[4], rvx.at[e - 1, 1], at_x(e)))
    for copy in vx_in:
        copy.wait_recv()
    mine = pl.ds(pl.multiple_of(r * 64, 64), 64)
    u[0, mine] = sv2[x] + rvx[0, 0] + rvx[1, 0] + rvx[2, 0]
    u[1, mine] = sv2[4] + rvx[0, 1] + rvx[1, 1] + rvx[2, 1]
    uz_in = put(u.at[:, mine], u.at[:, mine], z_near)
    uz_in.wait_recv()
    pair = pl.ds(pl.multiple_of(y * 128, 128), 128)
    uy_in = [put(u.at[:, pair], u.at[:, pair], at_y(d)) for d in (2, 1, 3)]

    for d in (2, 1, 3):
        p_in[d].wait_recv()
    for j in range(5):
        s[j] = p[0, j] + ry[0, j] + ry[1, j] + ry[2, j]
    z_sum = put(s.at[:, pl.ds(pl.multiple_of((1 - zlo) * 128, 128), 128), :], rz, z_near)

    for copy in uy_in:
        copy.wait_recv()
    g[k] = u[1, 256:512]
    g_in = put(g.at[k], g.at[k], sibling)

    z_sum.wait_recv()
    s2[...] = s[:, pl.ds(pl.multiple_of(zlo * 128, 128), 128), :] + rz[...]
    x_sum = []
    for e in (2, 1, 3):
        x_sum.append(put(s2.at[4], rx.at[e - 1, 1], at_x(e)))
        x_sum.append(put(s2.at[(x + e) % 4], rx.at[e - 1, 0], at_x(e)))

    g_in.wait_recv()
    middle_second = exact(t2_ref[...], u[0, 0:256])
    inner_first = (
        u[0, 256:512] - exact(g[0], middle_second[:128]) - exact(g[1], middle_second[128:])
    )
    middle_first = exact(t1_ref[...], inner_first)

    for copy in x_sum:
        copy.wait_recv()
    xv[q] = s2[4] + rx[0, 1] + rx[1, 1] + rx[2, 1]
    far_in = put(xv.at[q], xv.at[q], z_far)
    sib_in = put(xv.at[q], xv.at[q], sibling)
    total = s2[x] + rx[0, 0] + rx[1, 0] + rx[2, 0]
    far_in.wait_recv()
    pass_in = put(xv.at[far], xv.at[far], sibling)
    sib_in.wait_recv()
    pass_in.wait_recv()
    for j in range(4):
        middle = middle_second if j < 2 else middle_first
        total = total - exact(xv[j], middle[(j % 2) * 128 : (j % 2 + 1) * 128])
    out_ref[...] = total * lax.rsqrt(ev_ref[...])

    for copy in started:
        copy.wait_send()


def per_device(tokens, eigvecs, eigvals, v_first, v_second, t_first, t_second):
    vmem = pl.BlockSpec(memory_space=pltpu.VMEM)
    return pl.pallas_call(
        kernel,
        out_shape=jax.ShapeDtypeStruct((128, 128), F32),
        in_specs=[vmem] * 7,
        out_specs=vmem,
        scratch_shapes=[
            pltpu.VMEM((3, 8, YSEG), BF16),
            pltpu.VMEM((4, 4, 8, ROWS), BF16),
            pltpu.VMEM((4, 2, 4, 2, 2, 8, ROWS), BF16),
            pltpu.VMEM((256, ROWS), BF16),
            pltpu.VMEM((SLAB, 128), BF16),
            pltpu.VMEM((ROWS, 512), BF16),
            pltpu.VMEM((2, 4, 4, OWN, 128), BF16),
            pltpu.VMEM((2, 512, ROWS), BF16),
            pltpu.VMEM((ROWS, 256), BF16),
            pltpu.VMEM((ROWS, 256), BF16),
            pltpu.VMEM((4, 5, 256, 128), F32),
            pltpu.VMEM((3, 5, 256, 128), F32),
            pltpu.VMEM((5, 256, 128), F32),
            pltpu.VMEM((5, 128, 128), F32),
            pltpu.VMEM((5, 128, 128), F32),
            pltpu.VMEM((3, 2, 128, 128), F32),
            pltpu.VMEM((4, 128, 128), F32),
            pltpu.VMEM((5, 512, 128), F32),
            pltpu.VMEM((3, 5, 128, 128), F32),
            pltpu.VMEM((5, 128, 128), F32),
            pltpu.VMEM((5, 64, 128), F32),
            pltpu.VMEM((5, 64, 128), F32),
            pltpu.VMEM((3, 2, 64, 128), F32),
            pltpu.VMEM((2, 512, 128), F32),
            pltpu.VMEM((2, 256, 128), F32),
            pltpu.SemaphoreType.DMA((COPIES,)),
            pltpu.SemaphoreType.DMA((COPIES,)),
            pltpu.SemaphoreType.DMA((16,)),
        ],
        compiler_params=pltpu.CompilerParams(
            collective_id=0, has_side_effects=True, vmem_limit_bytes=56 * 1024 * 1024
        ),
    )(tokens, eigvecs, v_first, v_second, t_first, t_second, eigvals.reshape(1, 128))


def solution(mesh):
    in_specs = (
        P(("row", "col"), None),
        P("row", "col"),
        P("col"),
        P(("row", "col"), None),
        P(("row", "col"), None),
        P(),
        P(),
    )
    out_specs = P("row", "col")
    return jax.shard_map(
        per_device, mesh=mesh, in_specs=in_specs, out_specs=out_specs, check_vma=False
    )
```

time: 655 us -> 116 us (0.18)
  waiting for transfers between devices: 528 us -> 0 us
  Pallas kernels: 0 us -> 115 us
  matrix products: 58.7 us -> 0 us
  local copies, waits for them, and re-layouts: 42.7 us -> 1.47 us
  between operations: 13.5 us -> 0.01 us
    psum x2 -> x0, waiting for transfers between devices: 276 us -> none  [per_device(): inner = lax.psum(partial_inner(panel, block), 'row')]
    all_gather x3 -> x0, waiting for transfers between devices: 213 us -> none  [the longest x1 80.9 us: per_device(): row_tokens = lax.all_gather(tokens, 'col', axis=0, tiled=True)]
    pallas_call x0 -> x1, Pallas kernels: none -> 115 us  [per_device(): pl.pallas_call(kernel, out_shape=jax.ShapeDtypeStruct((128, 128), F32), i...]
    dot_general x7 -> x0, matrix products: 58.7 us -> none  [the longest x2 23.4 us: local_update(): jnp.dot(panel, middle, precision=lax.Precision.HIGHEST, preferred_element...]
    reduce_scatter x1 -> x0, waiting for transfers between devices: 37.5 us -> none  [per_device(): lax.psum_scatter(partial_value, 'row', scatter_dimension=0, tiled=True)]
    all_gather x1 -> x0, local copies, waits for them, and re-layouts: 18.4 us -> none  [per_device(): row_tokens = lax.all_gather(tokens, 'col', axis=0, tiled=True)]
    all_to_all x1 -> x0, local copies, waits for them, and re-layouts: 17.6 us -> none  [per_device(): lax.all_to_all(row_tokens, 'row', split_axis=1, concat_axis=0, tiled=True)]
  transfers between devices with their start and end apart: 7 -> 0, of which waited for: 6 -> 0; matrix products, arithmetic and copies ran while one was open for 11% -> 0% of each run, Pallas kernels for 0% -> 0%
where the time goes in v1:
time: 116 us
  Pallas kernels  115 us (99%)
  local copies, waits for them, and re-layouts  1.47 us (1%)
    pallas_call x1, Pallas kernels, per_device(): pl.pallas_call(kernel, out_shape=jax.ShapeDtypeStruct((128, 128), F32), i...  115 us

profile of v1, /device:TPU:1, one launch (start us, length us, event | category | flops | bytes accessed | tf_op | source)
XLA Modules:
  0.0 116.1 jit_solution(8847098718515477821)
XLA Ops:
  0.0 114.6 %shard_map.73 = f32[128,128]{1,0:T(8,128)} custom-call(bf16[8,53248]{1,0:T(8,128)(2,1)} %x_ref.1, f32[6656,128]{1,0:T(8,128)} %e_ref.1, f32[416,256]{1,0:T(8,128)} %v1_ref.1, f32[416,256]{1,0:T(8,128)} %v2_ref.1, f32[256,256]{1,0:T(8,128)} %t1_ref.1, f32[256,256]{1,0:T(8,128)} %t2_ref.1, f32[1,128]{1,0:T(1,128)} %bitcast.1), custom_call_target="tpu_custom_call" | custom-call | tf_op jit(solution)/shard_map/pallas_call | solution.py:272
  114.6 1.5 %copy.9 = f32[128,128]{1,0:T(8,128)} copy(f32[128,128]{1,0:T(8,128)} %shard_map.73) | data formatting | bytes 131072

commit v2 on v1

v2 whole, which is shorter than its diff:
```python
import functools

import jax
import jax.numpy as jnp
from jax import lax
from jax.experimental import pallas as pl
from jax.experimental.pallas import tpu as pltpu
from jax.sharding import PartitionSpec as P

MESH = pl.DeviceIdType.MESH
BF16 = jnp.bfloat16
F32 = jnp.float32
HIGH = lax.Precision.HIGHEST

ROWS = 1664
OWN = 416
SLAB = 6656
YSEG = 2 * SLAB
HALF = ROWS // 2
COPIES = 120


def mm(a, b):
    return jnp.dot(a, b, preferred_element_type=F32)


def exact(a, b):
    return jnp.dot(a, b, precision=HIGH, preferred_element_type=F32)


def kernel(
    x_ref, e_ref, v1_ref, v2_ref, t1_ref, t2_ref, ev_ref, out_ref,
    xy, xs, xb, x2, es, eb, vb, vt, vq, vc,
    pa, ra, sa, rxa, pb, rb, sb, ryb, ab, rab,
    px, rx, sx, rzx, s2x, rx2, xv,
    va, rva, sva, rvxa, vbp, rvb, svb, rvyb, vv, rvv, svv, rvx,
    uz, ruz, u, g,
    send, recv, local,
):
    r, c = lax.axis_index("row"), lax.axis_index("col")
    y, zlo = r // 2, r % 2
    x, q = c // 4, c % 4
    zhi, k = q // 2, q % 2

    def at_y(d):
        return (((y + d) % 4) * 2 + zlo, c)

    def at_x(d):
        return (r, ((x + d) % 4) * 4 + q)

    z_far = (r, x * 4 + (1 - zhi) * 2 + k)
    z_near = (y * 2 + 1 - zlo, c)
    z_other = (y * 2 + 1 - zlo, x * 4 + (1 - zhi) * 2 + k)
    sibling = (r, x * 4 + zhi * 2 + 1 - k)

    peers = [at_y(1), at_y(2), at_y(3), at_x(1), at_x(2), at_x(3)]
    peers += [z_far, z_near, z_other, sibling]
    barrier = pltpu.get_barrier_semaphore()
    for peer in peers:
        pl.semaphore_signal(barrier, inc=1, device_id=peer, device_id_type=MESH)

    started = []

    def put(src, dst, device):
        slot = len(started)
        copy = pltpu.make_async_remote_copy(
            src_ref=src, dst_ref=dst, send_sem=send.at[slot], recv_sem=recv.at[slot],
            device_id=device, device_id_type=MESH,
        )
        copy.start()
        started.append(copy)
        return copy

    here = []

    def move(src, dst):
        copy = pltpu.make_async_copy(src, dst, local.at[len(here)])
        copy.start()
        here.append(copy)
        return copy

    def arrived(copies):
        for copy in copies:
            copy.wait_recv()

    def rows(start, size):
        return pl.ds(pl.multiple_of(start, size), size)

    for chunk in range(4):
        panel = v2_ref if chunk < 2 else v1_ref
        value = panel[:, (chunk % 2) * 128 : (chunk % 2 + 1) * 128]
        high = value.astype(BF16)
        vb[0, chunk, q] = high
        vb[1, chunk, q] = (value - high.astype(F32)).astype(BF16)

    def cast(i, carry):
        at = rows(i * 208, 208)
        es[at] = e_ref[at].astype(BF16)
        return carry

    lax.fori_loop(0, 32, cast, 0)

    pl.semaphore_wait(barrier, len(peers))

    y_in = {}
    for d in (2, 1, 3):
        to = (y + d) % 4
        src = x_ref.at[:, pl.ds(pl.multiple_of(to * YSEG, 128), YSEG)]
        y_in[d] = put(src, xy.at[d - 1], at_y(d))
    v_far = put(vb.at[:, :, q], vb.at[:, :, q], z_far)
    v_sib = put(vb.at[:, :, q], vb.at[:, :, q], sibling)

    def x_stage(d):
        def piece(zl, to):
            at = zl * SLAB + to * ROWS
            if d == 0:
                return x_ref.at[:, pl.ds(pl.multiple_of(y * YSEG + at, 128), ROWS)]
            return xy.at[d - 1, :, pl.ds(pl.multiple_of(at, 128), ROWS)]

        mine, other = xb.at[d, zlo, x, zhi, k], xs.at[d, x]
        waits = []
        for e in (2, 1, 3):
            to = (x + e) % 4
            waits.append(put(piece(zlo, to), mine, at_x(e)))
            waits.append(put(piece(1 - zlo, to), other, at_x(e)))
        return waits, [move(piece(zlo, x), mine), move(piece(1 - zlo, x), other)]

    own_cols = rows(x * 128, 128)

    def e_stage(half):
        waits = []
        for e in (2, 1, 3):
            src = es.at[rows(((x + e) % 4 * 2 + half) * HALF, HALF)]
            waits.append(put(src, eb.at[half * HALF : (half + 1) * HALF, own_cols], at_x(e)))
        return waits

    def z_stage(d):
        block = xb.at[d, zlo, :, zhi, k]
        return [
            put(block, block, z_far),
            put(xs.at[d], block, z_near),
            put(xs.at[d], block, z_other),
        ]

    x_in, z_in, c_in = {}, {}, {}
    x_in[0] = x_stage(0)
    e_in = e_stage(0)
    e_own = move(es.at[rows(x * ROWS, ROWS)], eb.at[:, own_cols])
    for d in (2, 1, 3):
        y_in[d].wait_recv()
        x_in[d] = x_stage(d)
    order = (2, 1, 3, 0)
    for d in order:
        arrived(x_in[d][0])
        for copy in x_in[d][1]:
            copy.wait()
        z_in[d] = z_stage(d)
        if d == 2:
            e_in += e_stage(1)

    v_far.wait_recv()
    far = (1 - zhi) * 2 + k
    v_pass = put(vb.at[:, :, far], vb.at[:, :, far], sibling)
    v_sib.wait_recv()
    v_pass.wait_recv()

    for term in range(2):
        vq[:, term * 128 : (term + 1) * 128] = vb[term, q].reshape(ROWS, 128)
        vc[:, term * 128 : (term + 1) * 128] = vb[term, k].reshape(ROWS, 128)
        for chunk in range(4):
            vt[term, chunk * 128 : (chunk + 1) * 128, :] = vb[term, chunk].reshape(ROWS, 128).T
    both = mm(vt[0], vc[...])
    vv[...] = both[:, :128] + both[:, 128:] + mm(vt[1], vc[:, :128])
    vv_in = [
        put(vv.at[rows((y - d) % 4 * 128, 128)], rvv.at[d - 1], at_y(-d)) for d in (2, 1, 3)
    ]

    def forward(d):
        arrived(z_in[d])
        block = xb.at[d, :, :, :, k]
        c_in[d] = put(block, block, sibling)

    def project_panel(d):
        c_in[d].wait_recv()

        def pack(i, carry):
            value = xb[d, i // 4, i % 4].astype(F32).reshape(32, ROWS)
            x2[d, rows(i * 32, 32)] = value.astype(BF16)
            return carry

        lax.fori_loop(0, 8, pack, 0)
        both = mm(x2[d], vq[...])
        px[d] = both[:, :128] + both[:, 128:]
        if d > 0:
            return put(px.at[d], rx.at[d - 1], at_y(-d))

    def project(d):
        part = mm(x2[d], eb[...])
        for j in range(4):
            pa[d, j] = part[:128, j * 128 : (j + 1) * 128]
            pb[d, j] = part[128:, j * 128 : (j + 1) * 128]
        if d > 0:
            a_in.append(put(pa.at[d], ra.at[d - 1], at_y(-d)))
        b_in[d] = [put(pb.at[d, (x + e) % 4], rb.at[e - 1, d], at_x(e)) for e in (2, 1, 3)]

    px_in, a_in, b_in = [], [], {}
    forward(2)
    px_in.append(project_panel(2))

    arrived(vv_in)
    svv[...] = vv[rows(y * 128, 128)] + rvv[0] + rvv[1] + rvv[2]
    vvx_in = [put(svv, rvx.at[e - 1], at_x(e)) for e in (2, 1, 3)]

    forward(1)
    px_in.append(project_panel(1))

    arrived(e_in)
    e_own.wait()
    project(2)

    for half in range(2):
        cols = eb[:, half * 256 : (half + 1) * 256]
        part = mm(vt[0], cols) + mm(vt[1], cols)
        for j in range(2):
            for chunk in range(4):
                tile = part[chunk * 128 : (chunk + 1) * 128, j * 128 : (j + 1) * 128]
                va[chunk, 2 * half + j] = tile[:64]
                vbp[2 * half + j, chunk] = tile[64:]
    va_in = [put(va.at[(y - d) % 4], rva.at[d - 1], at_y(-d)) for d in (2, 1, 3)]
    vb_in = [put(vbp.at[(x + e) % 4], rvb.at[e - 1], at_x(e)) for e in (2, 1, 3)]

    project(1)
    forward(3)
    px_in.append(project_panel(3))
    project(3)
    forward(0)
    project_panel(0)
    project(0)

    arrived(px_in)
    sx[...] = px[0] + rx[0] + rx[1] + rx[2]
    xz_in = put(sx.at[rows((1 - zlo) * 128, 128)], rzx, z_near)

    arrived(va_in)
    sva[...] = va[y] + rva[0] + rva[1] + rva[2]
    va2_in = [put(sva.at[(x + e) % 4], rvxa.at[e - 1], at_x(e)) for e in (2, 1, 3)]
    arrived(vb_in)
    svb[...] = vbp[x] + rvb[0] + rvb[1] + rvb[2]
    vb2_in = [put(svb.at[(y - d) % 4], rvyb.at[d - 1], at_y(-d)) for d in (2, 1, 3)]

    xz_in.wait_recv()
    s2x[...] = sx[rows(zlo * 128, 128)] + rzx[...]
    xx_in = [put(s2x, rx2.at[e - 1], at_x(e)) for e in (2, 1, 3)]

    b2_in = []
    for d in order:
        arrived(b_in[d])
        sb[d] = pb[d, x] + rb[0, d] + rb[1, d] + rb[2, d]
        if d > 0:
            b2_in.append(put(sb.at[d], ryb.at[d - 1], at_y(-d)))

    arrived(vvx_in)
    uz[1] = svv[...] + rvx[0] + rvx[1] + rvx[2]
    arrived(va2_in)
    uz[0, :64] = sva[x] + rvxa[0] + rvxa[1] + rvxa[2]
    arrived(vb2_in)
    uz[0, 64:] = svb[y] + rvyb[0] + rvyb[1] + rvyb[2]
    uz_in = put(uz, ruz, z_near)

    arrived(a_in)
    for j in range(4):
        sa[j] = pa[0, j] + ra[0, j] + ra[1, j] + ra[2, j]
    a2_in = [put(sa.at[(x + e) % 4], rxa.at[e - 1], at_x(e)) for e in (2, 1, 3)]

    arrived(xx_in)
    xv[q] = s2x[...] + rx2[0] + rx2[1] + rx2[2]
    far_in = put(xv.at[q], xv.at[q], z_far)
    sib_in = put(xv.at[q], xv.at[q], sibling)

    uz_in.wait_recv()
    own = rows(y * 128, 128)
    u[:, own] = uz[...] + ruz[...]
    uy_in = [put(u.at[:, own], u.at[:, own], at_y(d)) for d in (2, 1, 3)]

    arrived(b2_in)
    ab[1] = sb[0] + ryb[0] + ryb[1] + ryb[2]
    arrived(a2_in)
    ab[0] = sa[x] + rxa[0] + rxa[1] + rxa[2]
    ab_in = put(ab.at[1 - zlo], rab, z_near)

    far_in.wait_recv()
    pass_in = put(xv.at[far], xv.at[far], sibling)

    arrived(uy_in)
    g[k] = u[1, 256:512]
    g_in = put(g.at[k], g.at[k], sibling)
    middle_second = exact(t2_ref[...], u[0, 0:256])
    g_in.wait_recv()
    inner_first = (
        u[0, 256:512] - exact(g[0], middle_second[:128]) - exact(g[1], middle_second[128:])
    )
    middle_first = exact(t1_ref[...], inner_first)

    sib_in.wait_recv()
    pass_in.wait_recv()
    total = jnp.zeros((128, 128), F32)
    for j in range(4):
        middle = middle_second if j < 2 else middle_first
        total += exact(xv[j], middle[(j % 2) * 128 : (j % 2 + 1) * 128])
    ab_in.wait_recv()
    out_ref[...] = (ab[zlo] + rab[...] - total) * lax.rsqrt(ev_ref[...])

    for copy in started:
        copy.wait_send()


def per_device(tokens, eigvecs, eigvals, v_first, v_second, t_first, t_second):
    vmem = pl.BlockSpec(memory_space=pltpu.VMEM)
    return pl.pallas_call(
        kernel,
        out_shape=jax.ShapeDtypeStruct((128, 128), F32),
        in_specs=[vmem] * 7,
        out_specs=vmem,
        scratch_shapes=[
            pltpu.VMEM((3, 8, YSEG), BF16),
            pltpu.VMEM((4, 4, 8, ROWS), BF16),
            pltpu.VMEM((4, 2, 4, 2, 2, 8, ROWS), BF16),
            pltpu.VMEM((4, 256, ROWS), BF16),
            pltpu.VMEM((SLAB, 128), BF16),
            pltpu.VMEM((ROWS, 512), BF16),
            pltpu.VMEM((2, 4, 4, OWN, 128), BF16),
            pltpu.VMEM((2, 512, ROWS), BF16),
            pltpu.VMEM((ROWS, 256), BF16),
            pltpu.VMEM((ROWS, 256), BF16),
            pltpu.VMEM((4, 4, 128, 128), F32),
            pltpu.VMEM((3, 4, 128, 128), F32),
            pltpu.VMEM((4, 128, 128), F32),
            pltpu.VMEM((3, 128, 128), F32),
            pltpu.VMEM((4, 4, 128, 128), F32),
            pltpu.VMEM((3, 4, 128, 128), F32),
            pltpu.VMEM((4, 128, 128), F32),
            pltpu.VMEM((3, 128, 128), F32),
            pltpu.VMEM((2, 128, 128), F32),
            pltpu.VMEM((128, 128), F32),
            pltpu.VMEM((4, 256, 128), F32),
            pltpu.VMEM((3, 256, 128), F32),
            pltpu.VMEM((256, 128), F32),
            pltpu.VMEM((128, 128), F32),
            pltpu.VMEM((128, 128), F32),
            pltpu.VMEM((3, 128, 128), F32),
            pltpu.VMEM((4, 128, 128), F32),
            pltpu.VMEM((4, 4, 64, 128), F32),
            pltpu.VMEM((3, 4, 64, 128), F32),
            pltpu.VMEM((4, 64, 128), F32),
            pltpu.VMEM((3, 64, 128), F32),
            pltpu.VMEM((4, 4, 64, 128), F32),
            pltpu.VMEM((3, 4, 64, 128), F32),
            pltpu.VMEM((4, 64, 128), F32),
            pltpu.VMEM((3, 64, 128), F32),
            pltpu.VMEM((512, 128), F32),
            pltpu.VMEM((3, 128, 128), F32),
            pltpu.VMEM((128, 128), F32),
            pltpu.VMEM((3, 128, 128), F32),
            pltpu.VMEM((2, 128, 128), F32),
            pltpu.VMEM((2, 128, 128), F32),
            pltpu.VMEM((2, 512, 128), F32),
            pltpu.VMEM((2, 256, 128), F32),
            pltpu.SemaphoreType.DMA((COPIES,)),
            pltpu.SemaphoreType.DMA((COPIES,)),
            pltpu.SemaphoreType.DMA((16,)),
        ],
        compiler_params=pltpu.CompilerParams(
            collective_id=0, has_side_effects=True, vmem_limit_bytes=56 * 1024 * 1024
        ),
    )(tokens, eigvecs, v_first, v_second, t_first, t_second, eigvals.reshape(1, 128))


def solution(mesh):
    in_specs = (
        P(("row", "col"), None),
        P("row", "col"),
        P("col"),
        P(("row", "col"), None),
        P(("row", "col"), None),
        P(),
        P(),
    )
    out_specs = P("row", "col")
    return jax.shard_map(
        per_device, mesh=mesh, in_specs=in_specs, out_specs=out_specs, check_vma=False
    )
```

time: 116 us -> 86.5 us (0.75)
  Pallas kernels: 115 us -> 84.2 us
    pallas_call x1, Pallas kernels: 115 us -> 84.2 us  [per_device(): pl.pallas_call(kernel, out_shape=jax.ShapeDtypeStruct((128, 128), F32), i...]
where the time goes in v2:
time: 86.5 us; the launch traced here: 85.7 us
  Pallas kernels  84.2 us (97%)
  local copies, waits for them, and re-layouts  1.47 us (2%)
    pallas_call x1, Pallas kernels, per_device(): pl.pallas_call(kernel, out_shape=jax.ShapeDtypeStruct((128, 128), F32), i...  84.2 us

profile of v2, /device:TPU:1, one launch (start us, length us, event | category | flops | bytes accessed | tf_op | source)
XLA Modules:
  0.0 85.7 jit_solution(14905381192879608498)
XLA Ops:
  0.0 84.2 %shard_map.73 = f32[128,128]{1,0:T(8,128)} custom-call(bf16[8,53248]{1,0:T(8,128)(2,1)} %x_ref.1, f32[6656,128]{1,0:T(8,128)} %e_ref.1, f32[416,256]{1,0:T(8,128)} %v1_ref.1, f32[416,256]{1,0:T(8,128)} %v2_ref.1, f32[256,256]{1,0:T(8,128)} %t1_ref.1, f32[256,256]{1,0:T(8,128)} %t2_ref.1, f32[1,128]{1,0:T(1,128)} %bitcast.1), custom_call_target="tpu_custom_call" | custom-call | tf_op jit(solution)/shard_map/pallas_call | solution.py:319
  84.2 1.5 %copy.9 = f32[128,128]{1,0:T(8,128)} copy(f32[128,128]{1,0:T(8,128)} %shard_map.73) | data formatting | bytes 131072

commit v3 on v2

v3 whole, which is shorter than its diff:
```python
import functools

import jax
import jax.numpy as jnp
from jax import lax
from jax.experimental import pallas as pl
from jax.experimental.pallas import tpu as pltpu
from jax.sharding import PartitionSpec as P

MESH = pl.DeviceIdType.MESH
BF16 = jnp.bfloat16
F32 = jnp.float32
HIGH = lax.Precision.HIGHEST

ROWS = 1664
OWN = 416
SLAB = 6656
YSEG = 2 * SLAB
HALF = ROWS // 2
COPIES = 128


def mm(a, b):
    return jnp.dot(a, b, preferred_element_type=F32)


def exact(a, b):
    return jnp.dot(a, b, precision=HIGH, preferred_element_type=F32)


def kernel(
    x_ref, e_ref, v1_ref, v2_ref, t1_ref, t2_ref, out_ref,
    xy, xs, xb, x2, ef, es, eb, vb, vt, vq, vc,
    pa, ha, ra, sa, rxa, pb, rb, sb, ryb, ab, rab,
    px, hx, rx, sx, rzx, s2x, rx2, xv,
    va, hva, rva, sva, rvxa, vbp, rvb, svb, rvyb, uz, ruz, u,
    vv, rvv, svv, rvx, uv, ruv, g,
    send, recv, local,
):
    r, c = lax.axis_index("row"), lax.axis_index("col")
    y, zlo = r // 2, r % 2
    x, q = c // 4, c % 4
    zhi, k = q // 2, q % 2

    def at_y(d):
        return (((y + d) % 4) * 2 + zlo, c)

    def at_x(d):
        return (r, ((x + d) % 4) * 4 + q)

    z_far = (r, x * 4 + (1 - zhi) * 2 + k)
    z_near = (y * 2 + 1 - zlo, c)
    z_other = (y * 2 + 1 - zlo, x * 4 + (1 - zhi) * 2 + k)
    sibling = (r, x * 4 + zhi * 2 + 1 - k)

    peers = [at_y(1), at_y(2), at_y(3), at_x(1), at_x(2), at_x(3)]
    peers += [z_far, z_near, z_other, sibling]
    barrier = pltpu.get_barrier_semaphore()
    for peer in peers:
        pl.semaphore_signal(barrier, inc=1, device_id=peer, device_id_type=MESH)

    started = []

    def put(src, dst, device):
        slot = len(started)
        copy = pltpu.make_async_remote_copy(
            src_ref=src, dst_ref=dst, send_sem=send.at[slot], recv_sem=recv.at[slot],
            device_id=device, device_id_type=MESH,
        )
        copy.start()
        started.append(copy)
        return copy

    here = []

    def move(src, dst):
        copy = pltpu.make_async_copy(src, dst, local.at[len(here)])
        copy.start()
        here.append(copy)
        return copy

    def arrived(copies):
        for copy in copies:
            copy.wait_recv()

    def rows(start, size):
        return pl.ds(pl.multiple_of(start, size), size)

    loads = [move(e_ref.at[rows(i * ROWS, ROWS)], ef.at[rows(i * ROWS, ROWS)]) for i in range(4)]

    for chunk in range(4):
        panel = v2_ref if chunk < 2 else v1_ref
        value = panel[:, (chunk % 2) * 128 : (chunk % 2 + 1) * 128]
        high = value.astype(BF16)
        vb[0, chunk, q] = high
        vb[1, chunk, q] = (value - high.astype(F32)).astype(BF16)

    pl.semaphore_wait(barrier, len(peers))

    y_in = {}
    for d in (2, 1, 3):
        to = (y + d) % 4
        src = x_ref.at[:, pl.ds(pl.multiple_of(to * YSEG, 128), YSEG)]
        y_in[d] = put(src, xy.at[d - 1], at_y(d))
    v_far = put(vb.at[:, :, q], vb.at[:, :, q], z_far)
    v_sib = put(vb.at[:, :, q], vb.at[:, :, q], sibling)

    def x_stage(d):
        def piece(zl, to):
            at = zl * SLAB + to * ROWS
            if d == 0:
                return x_ref.at[:, pl.ds(pl.multiple_of(y * YSEG + at, 128), ROWS)]
            return xy.at[d - 1, :, pl.ds(pl.multiple_of(at, 128), ROWS)]

        mine, other = xb.at[d, zlo, x, zhi, k], xs.at[d, x]
        waits = []
        for e in (2, 1, 3):
            to = (x + e) % 4
            waits.append(put(piece(zlo, to), mine, at_x(e)))
            waits.append(put(piece(1 - zlo, to), other, at_x(e)))
        return waits, [move(piece(zlo, x), mine), move(piece(1 - zlo, x), other)]

    own_cols = rows(x * 128, 128)

    def e_stage(half):
        waits = []
        for e in (2, 1, 3):
            src = es.at[rows(((x + e) % 4 * 2 + half) * HALF, HALF)]
            waits.append(put(src, eb.at[half * HALF : (half + 1) * HALF, own_cols], at_x(e)))
        return waits

    def z_stage(d):
        block = xb.at[d, zlo, :, zhi, k]
        return [
            put(block, block, z_far),
            put(xs.at[d], block, z_near),
            put(xs.at[d], block, z_other),
        ]

    x_in, z_in, c_in = {}, {}, {}
    x_in[0] = x_stage(0)

    def cast(i, carry):
        at = rows(i * 208, 208)
        es[at] = ef[at].astype(BF16)
        return carry

    def keep(i, carry):
        eb[rows(i * 208, 208), own_cols] = es[rows(x * ROWS + i * 208, 208)]
        return carry

    for copy in loads:
        copy.wait()
    lax.fori_loop(0, 32, cast, 0)
    e_in = e_stage(0)
    lax.fori_loop(0, 8, keep, 0)
    y_in[2].wait_recv()
    x_in[2] = x_stage(2)
    for d in (1, 3):
        y_in[d].wait_recv()
        x_in[d] = x_stage(d)

    def along_z(d):
        arrived(x_in[d][0])
        for copy in x_in[d][1]:
            copy.wait()
        z_in[d] = z_stage(d)

    for d in (2, 1, 3, 0):
        along_z(d)
        if d == 2:
            e_in += e_stage(1)

    def forward(d):
        arrived(z_in[d])
        block = xb.at[d, :, :, :, k]
        c_in[d] = put(block, block, sibling)

    def halves(value, got):
        half = value.shape[0] // 2
        return {
            1: put(value.at[:half], got.at[0], at_y(-1)),
            3: put(value.at[half:], got.at[1], at_y(1)),
        }

    def project_panel(d):
        c_in[d].wait_recv()

        def pack(i, carry):
            value = xb[d, i // 4, i % 4].astype(F32).reshape(32, ROWS)
            x2[d, rows(i * 32, 32)] = value.astype(BF16)
            return carry

        lax.fori_loop(0, 8, pack, 0)
        both = mm(x2[d], vq[...])
        px[d] = both[:, :128] + both[:, 128:]

    def send_panel(d):
        x_half[d].wait_recv()
        if d == 1:
            px[1, :128] += hx[0]
            return put(px.at[1], rx.at[0], at_y(-1))
        px[3, 128:] += hx[1]
        return put(px.at[3], rx.at[1], at_y(1))

    def project(d):
        part = mm(x2[d], eb[...])
        for j in range(4):
            pa[d, j] = part[:128, j * 128 : (j + 1) * 128]
            pb[d, j] = part[128:, j * 128 : (j + 1) * 128]
        b_in[d] = [put(pb.at[d, (x + e) % 4], rb.at[e - 1, d], at_x(e)) for e in (2, 1, 3)]

    def send_lower(d):
        a_half[d].wait_recv()
        if d == 1:
            pa[1, :2] += ha[0]
            return put(pa.at[1], ra.at[0], at_y(-1))
        pa[3, 2:] += ha[1]
        return put(pa.at[3], ra.at[1], at_y(1))

    v_far.wait_recv()
    far = (1 - zhi) * 2 + k
    v_pass = put(vb.at[:, :, far], vb.at[:, :, far], sibling)
    forward(2)
    v_sib.wait_recv()
    v_pass.wait_recv()

    for term in range(2):
        vq[:, term * 128 : (term + 1) * 128] = vb[term, q].reshape(ROWS, 128)
        vc[:, term * 128 : (term + 1) * 128] = vb[term, k].reshape(ROWS, 128)
        for chunk in range(4):
            vt[term, chunk * 128 : (chunk + 1) * 128, :] = vb[term, chunk].reshape(ROWS, 128).T
    block = rows(256 + zhi * 128, 128)
    both = mm(vt[0, block], vc[...])
    vv[...] = both[:, :128] + both[:, 128:] + mm(vt[1, block], vc[:, :128])
    vv_in = [put(vv.at[rows((y - d) % 4 * 32, 32)], rvv.at[d - 1], at_y(-d)) for d in (2, 1, 3)]

    arrived(e_in)
    for half in range(2):
        cols = eb[:, half * 256 : (half + 1) * 256]
        part = mm(vt[0], cols) + mm(vt[1], cols)
        for j in range(2):
            for chunk in range(4):
                tile = part[chunk * 128 : (chunk + 1) * 128, j * 128 : (j + 1) * 128]
                va[chunk, 2 * half + j] = tile[:64]
                vbp[2 * half + j, chunk] = tile[64:]
    v_half = halves(va.at[(y + 2) % 4], hva)
    vb_in = [put(vbp.at[(x + e) % 4], rvb.at[e - 1], at_x(e)) for e in (2, 1, 3)]

    px_in, a_in, b_in = [], [], {}
    forward(1)
    project_panel(2)
    x_half = halves(px.at[2], hx)
    project(2)
    a_half = halves(pa.at[2], ha)

    arrived(vv_in)
    svv[...] = vv[rows(y * 32, 32)] + rvv[0] + rvv[1] + rvv[2]
    vvx_in = [put(svv, rvx.at[e - 1], at_x(e)) for e in (2, 1, 3)]

    project_panel(1)
    forward(3)
    project(1)
    px_in.append(send_panel(1))

    v_half[1].wait_recv()
    va[(y + 3) % 4, :2] += hva[0]
    va_in = [put(va.at[(y + 3) % 4], rva.at[0], at_y(-1))]
    v_half[3].wait_recv()
    va[(y + 1) % 4, 2:] += hva[1]
    va_in.append(put(va.at[(y + 1) % 4], rva.at[1], at_y(1)))

    a_in.append(send_lower(1))

    project_panel(3)
    px_in.append(send_panel(3))
    forward(0)
    project(3)
    a_in.append(send_lower(3))

    arrived(vvx_in)
    uv[...] = svv[...] + rvx[0] + rvx[1] + rvx[2]
    uv_in = put(uv, ruv, z_near)

    project_panel(0)
    project(0)

    arrived(va_in)
    sva[...] = va[y] + rva[0] + rva[1]
    va2_in = [put(sva.at[(x + e) % 4], rvxa.at[e - 1], at_x(e)) for e in (2, 1, 3)]
    arrived(vb_in)
    svb[...] = vbp[x] + rvb[0] + rvb[1] + rvb[2]
    vb2_in = [put(svb.at[(y - d) % 4], rvyb.at[d - 1], at_y(-d)) for d in (2, 1, 3)]

    arrived(px_in)
    sx[...] = px[0] + rx[0] + rx[1]
    xz_in = put(sx.at[rows((1 - zlo) * 128, 128)], rzx, z_near)

    own = rows(y * 32, 32)
    uv_in.wait_recv()
    g[zhi, k, own] = uv[...] + ruv[...]
    gy_in = [put(g.at[zhi, k, own], g.at[zhi, k, own], at_y(d)) for d in (2, 1, 3)]

    b2_in = []
    for d in (2, 1, 3):
        arrived(b_in[d])
        sb[d] = pb[d, x] + rb[0, d] + rb[1, d] + rb[2, d]
        b2_in.append(put(sb.at[d], ryb.at[d - 1], at_y(-d)))

    xz_in.wait_recv()
    s2x[...] = sx[rows(zlo * 128, 128)] + rzx[...]
    xx_in = [put(s2x, rx2.at[e - 1], at_x(e)) for e in (2, 1, 3)]

    arrived(a_in)
    for j in range(4):
        sa[j] = pa[0, j] + ra[0, j] + ra[1, j]
    a2_in = [put(sa.at[(x + e) % 4], rxa.at[e - 1], at_x(e)) for e in (2, 1, 3)]

    arrived(va2_in)
    uz[:64] = sva[x] + rvxa[0] + rvxa[1] + rvxa[2]
    arrived(vb2_in)
    uz[64:] = svb[y] + rvyb[0] + rvyb[1] + rvyb[2]
    uz_in = put(uz, ruz, z_near)

    arrived(gy_in)
    g_far = put(g.at[zhi, k], g.at[zhi, k], z_far)
    g_sib = put(g.at[zhi, k], g.at[zhi, k], sibling)

    arrived(xx_in)
    xv[q] = s2x[...] + rx2[0] + rx2[1] + rx2[2]
    far_in = put(xv.at[q], xv.at[q], z_far)
    sib_in = put(xv.at[q], xv.at[q], sibling)

    uz_in.wait_recv()
    own = rows(y * 128, 128)
    u[own] = uz[...] + ruz[...]
    uy_in = [put(u.at[own], u.at[own], at_y(d)) for d in (2, 1, 3)]

    g_far.wait_recv()
    g_pass = put(g.at[1 - zhi, k], g.at[1 - zhi, k], sibling)

    arrived(b_in[0])
    arrived(b2_in)
    ab[1] = pb[0, x] + rb[0, 0] + rb[1, 0] + rb[2, 0] + ryb[0] + ryb[1] + ryb[2]

    arrived(a2_in)
    ab[0] = sa[x] + rxa[0] + rxa[1] + rxa[2]
    ab_in = put(ab.at[1 - zlo], rab, z_near)

    far_in.wait_recv()
    pass_in = put(xv.at[far], xv.at[far], sibling)

    arrived(uy_in)
    middle_second = exact(t2_ref[...], u[0:256])
    g_sib.wait_recv()
    g_pass.wait_recv()
    lower, upper = middle_second[:128], middle_second[128:]
    inner_first = u[256:512] - jnp.concatenate(
        [exact(g[i, 0], lower) + exact(g[i, 1], upper) for i in range(2)], axis=0
    )
    middle_first = exact(t1_ref[...], inner_first)

    sib_in.wait_recv()
    pass_in.wait_recv()
    total = jnp.zeros((128, 128), F32)
    for j in range(4):
        middle = middle_second if j < 2 else middle_first
        total += exact(xv[j], middle[(j % 2) * 128 : (j % 2 + 1) * 128])
    ab_in.wait_recv()
    out_ref[...] = ab[zlo] + rab[...] - total

    for copy in started:
        copy.wait_send()


def per_device(tokens, eigvecs, eigvals, v_first, v_second, t_first, t_second):
    vmem = pl.BlockSpec(memory_space=pltpu.VMEM)
    hbm = pl.BlockSpec(memory_space=pltpu.HBM)
    projected = pl.pallas_call(
        kernel,
        out_shape=jax.ShapeDtypeStruct((128, 128), F32),
        in_specs=[hbm, hbm] + [vmem] * 4,
        out_specs=vmem,
        scratch_shapes=[
            pltpu.VMEM((3, 8, YSEG), BF16),
            pltpu.VMEM((4, 4, 8, ROWS), BF16),
            pltpu.VMEM((4, 2, 4, 2, 2, 8, ROWS), BF16),
            pltpu.VMEM((4, 256, ROWS), BF16),
            pltpu.VMEM((SLAB, 128), F32),
            pltpu.VMEM((SLAB, 128), BF16),
            pltpu.VMEM((ROWS, 512), BF16),
            pltpu.VMEM((2, 4, 4, OWN, 128), BF16),
            pltpu.VMEM((2, 512, ROWS), BF16),
            pltpu.VMEM((ROWS, 256), BF16),
            pltpu.VMEM((ROWS, 256), BF16),
            pltpu.VMEM((4, 4, 128, 128), F32),
            pltpu.VMEM((2, 2, 128, 128), F32),
            pltpu.VMEM((2, 4, 128, 128), F32),
            pltpu.VMEM((4, 128, 128), F32),
            pltpu.VMEM((3, 128, 128), F32),
            pltpu.VMEM((4, 4, 128, 128), F32),
            pltpu.VMEM((3, 4, 128, 128), F32),
            pltpu.VMEM((4, 128, 128), F32),
            pltpu.VMEM((3, 128, 128), F32),
            pltpu.VMEM((2, 128, 128), F32),
            pltpu.VMEM((128, 128), F32),
            pltpu.VMEM((4, 256, 128), F32),
            pltpu.VMEM((2, 128, 128), F32),
            pltpu.VMEM((2, 256, 128), F32),
            pltpu.VMEM((256, 128), F32),
            pltpu.VMEM((128, 128), F32),
            pltpu.VMEM((128, 128), F32),
            pltpu.VMEM((3, 128, 128), F32),
            pltpu.VMEM((4, 128, 128), F32),
            pltpu.VMEM((4, 4, 64, 128), F32),
            pltpu.VMEM((2, 2, 64, 128), F32),
            pltpu.VMEM((2, 4, 64, 128), F32),
            pltpu.VMEM((4, 64, 128), F32),
            pltpu.VMEM((3, 64, 128), F32),
            pltpu.VMEM((4, 4, 64, 128), F32),
            pltpu.VMEM((3, 4, 64, 128), F32),
            pltpu.VMEM((4, 64, 128), F32),
            pltpu.VMEM((3, 64, 128), F32),
            pltpu.VMEM((128, 128), F32),
            pltpu.VMEM((128, 128), F32),
            pltpu.VMEM((512, 128), F32),
            pltpu.VMEM((128, 128), F32),
            pltpu.VMEM((3, 32, 128), F32),
            pltpu.VMEM((32, 128), F32),
            pltpu.VMEM((3, 32, 128), F32),
            pltpu.VMEM((32, 128), F32),
            pltpu.VMEM((32, 128), F32),
            pltpu.VMEM((2, 2, 128, 128), F32),
            pltpu.SemaphoreType.DMA((COPIES,)),
            pltpu.SemaphoreType.DMA((COPIES,)),
            pltpu.SemaphoreType.DMA((16,)),
        ],
        compiler_params=pltpu.CompilerParams(
            collective_id=0, has_side_effects=True, vmem_limit_bytes=56 * 1024 * 1024
        ),
    )(tokens, eigvecs, v_first, v_second, t_first, t_second)
    return projected * lax.rsqrt(eigvals)[None, :]


def solution(mesh):
    in_specs = (
        P(("row", "col"), None),
        P("row", "col"),
        P("col"),
        P(("row", "col"), None),
        P(("row", "col"), None),
        P(),
        P(),
    )
    out_specs = P("row", "col")
    return jax.shard_map(
        per_device, mesh=mesh, in_specs=in_specs, out_specs=out_specs, check_vma=False
    )
```

time: 86.5 us -> 77.1 us (0.89)
  Pallas kernels: 84.2 us -> 73.6 us
  other arithmetic: 0 us -> 1.48 us
    pallas_call x1, Pallas kernels: 84.2 us -> 73.6 us  [per_device(): pl.pallas_call(kernel, out_shape=jax.ShapeDtypeStruct((128, 128), F32), i...]
    mul x0 -> x1, other arithmetic: none -> 1.48 us  [per_device(): return projected * lax.rsqrt(eigvals)[None, :]]
    unnamed x1 -> x0, local copies, waits for them, and re-layouts: 1.47 us -> none
where the time goes in v3:
time: 77.1 us; the launch traced here: 75.7 us
  Pallas kernels  73.6 us (95%)
  other arithmetic  1.48 us (2%)
    pallas_call x1, Pallas kernels, per_device(): pl.pallas_call(kernel, out_shape=jax.ShapeDtypeStruct((128, 128), F32), i...  73.6 us

profile of v3, /device:TPU:1, one launch (start us, length us, event | category | flops | bytes accessed | tf_op | source)
XLA Modules:
  0.0 75.7 jit_solution(11721582620266187381)
XLA Ops:
  0.0 0.7 rsqrt.3
  0.7 73.6 %shard_map.73 = f32[128,128]{1,0:T(8,128)} custom-call(bf16[8,53248]{1,0:T(8,128)(2,1)} %x_ref.1, f32[6656,128]{1,0:T(8,128)} %e_ref.1, f32[416,256]{1,0:T(8,128)} %v1_ref.1, f32[416,256]{1,0:T(8,128)} %v2_ref.1, f32[256,256]{1,0:T(8,128)} %t1_ref.1, f32[256,256]{1,0:T(8,128)} %t2_ref.1), custom_call_target="tpu_custom_call" | custom-call | tf_op jit(solution)/shard_map/pallas_call | solution.py:379
  74.3 1.5 %broadcast_multiply_fusion = f32[128,128]{1,0:T(8,128)} fusion(f32[128,128]{1,0:T(8,128)} %shard_map.73, f32[128]{0:T(128)S(1)} %rsqrt.3), kind=kLoop, calls=%fused_computation | loop fusion | flops 16384 | bytes 131584 | tf_op jit(solution)/shard_map/mul | solution.py:442

commit v4 on v3

--- a/solution.py
+++ b/solution.py
@@ -247,10 +247,14 @@
     v_half = halves(va.at[(y + 2) % 4], hva)
     vb_in = [put(vbp.at[(x + e) % 4], rvb.at[e - 1], at_x(e)) for e in (2, 1, 3)]
 
+
     px_in, a_in, b_in = [], [], {}
+
     forward(1)
+
     project_panel(2)
     x_half = halves(px.at[2], hx)
+
     project(2)
     a_half = halves(pa.at[2], ha)
 
@@ -259,8 +263,11 @@
     vvx_in = [put(svv, rvx.at[e - 1], at_x(e)) for e in (2, 1, 3)]
 
     project_panel(1)
+
     forward(3)
+
     project(1)
+
     px_in.append(send_panel(1))
 
     v_half[1].wait_recv()
@@ -273,9 +280,13 @@
     a_in.append(send_lower(1))
 
     project_panel(3)
+
     px_in.append(send_panel(3))
+
     forward(0)
+
     project(3)
+
     a_in.append(send_lower(3))
 
     arrived(vvx_in)
@@ -283,7 +294,6 @@
     uv_in = put(uv, ruv, z_near)
 
     project_panel(0)
-    project(0)
 
     arrived(va_in)
     sva[...] = va[y] + rva[0] + rva[1]
@@ -291,6 +301,8 @@
     arrived(vb_in)
     svb[...] = vbp[x] + rvb[0] + rvb[1] + rvb[2]
     vb2_in = [put(svb.at[(y - d) % 4], rvyb.at[d - 1], at_y(-d)) for d in (2, 1, 3)]
+
+    project(0)
 
     arrived(px_in)
     sx[...] = px[0] + rx[0] + rx[1]

time: 77.1 us -> 76.3 us (0.990); the launches traced: 75.7 us -> 75.9 us
  no operation moved by 1% of the time
where the time goes in v4:
time: 76.3 us; the launch traced here: 75.9 us
  Pallas kernels  73.7 us (97%)
  other arithmetic  1.48 us (2%)
    pallas_call x1, Pallas kernels, per_device(): pl.pallas_call(kernel, out_shape=jax.ShapeDtypeStruct((128, 128), F32), i...  73.7 us

profile of v4, /device:TPU:1, one launch (start us, length us, event | category | flops | bytes accessed | tf_op | source)
XLA Modules:
  0.0 75.9 jit_solution(1474547510851526238)
XLA Ops:
  0.0 0.7 rsqrt.3
  0.7 73.7 %shard_map.73 = f32[128,128]{1,0:T(8,128)} custom-call(bf16[8,53248]{1,0:T(8,128)(2,1)} %x_ref.1, f32[6656,128]{1,0:T(8,128)} %e_ref.1, f32[416,256]{1,0:T(8,128)} %v1_ref.1, f32[416,256]{1,0:T(8,128)} %v2_ref.1, f32[256,256]{1,0:T(8,128)} %t1_ref.1, f32[256,256]{1,0:T(8,128)} %t2_ref.1), custom_call_target="tpu_custom_call" | custom-call | tf_op jit(solution)/shard_map/pallas_call | solution.py:391
  74.4 1.5 %broadcast_multiply_fusion = f32[128,128]{1,0:T(8,128)} fusion(f32[128,128]{1,0:T(8,128)} %shard_map.73, f32[128]{0:T(128)S(1)} %rsqrt.3), kind=kLoop, calls=%fused_computation | loop fusion | flops 16384 | bytes 131584 | tf_op jit(solution)/shard_map/mul | solution.py:454

commit v5 on v4

--- a/solution.py
+++ b/solution.py
@@ -248,6 +248,7 @@
     vb_in = [put(vbp.at[(x + e) % 4], rvb.at[e - 1], at_x(e)) for e in (2, 1, 3)]
 
 
+    first = len(started)
     px_in, a_in, b_in = [], [], {}
 
     forward(1)
@@ -313,15 +314,18 @@
     g[zhi, k, own] = uv[...] + ruv[...]
     gy_in = [put(g.at[zhi, k, own], g.at[zhi, k, own], at_y(d)) for d in (2, 1, 3)]
 
+    for copy in started[:first]:
+        copy.wait_send()
+
+    xz_in.wait_recv()
+    s2x[...] = sx[rows(zlo * 128, 128)] + rzx[...]
+    xx_in = [put(s2x, rx2.at[e - 1], at_x(e)) for e in (2, 1, 3)]
+
     b2_in = []
     for d in (2, 1, 3):
         arrived(b_in[d])
         sb[d] = pb[d, x] + rb[0, d] + rb[1, d] + rb[2, d]
         b2_in.append(put(sb.at[d], ryb.at[d - 1], at_y(-d)))
-
-    xz_in.wait_recv()
-    s2x[...] = sx[rows(zlo * 128, 128)] + rzx[...]
-    xx_in = [put(s2x, rx2.at[e - 1], at_x(e)) for e in (2, 1, 3)]
 
     arrived(a_in)
     for j in range(4):
@@ -381,7 +385,7 @@
     ab_in.wait_recv()
     out_ref[...] = ab[zlo] + rab[...] - total
 
-    for copy in started:
+    for copy in started[first:]:
         copy.wait_send()
 
 

time: 76.3 us -> 76.5 us (level)
  no operation moved by 1% of the time
where the time goes in v5:
time: 76.5 us; the launch traced here: 75.8 us
  Pallas kernels  73.6 us (96%)
  other arithmetic  1.48 us (2%)
    pallas_call x1, Pallas kernels, per_device(): pl.pallas_call(kernel, out_shape=jax.ShapeDtypeStruct((128, 128), F32), i...  73.6 us

profile of v5, /device:TPU:1, one launch (start us, length us, event | category | flops | bytes accessed | tf_op | source)
XLA Modules:
  0.0 75.8 jit_solution(2038196936532258172)
XLA Ops:
  0.0 0.7 rsqrt.3
  0.7 73.6 %shard_map.73 = f32[128,128]{1,0:T(8,128)} custom-call(bf16[8,53248]{1,0:T(8,128)(2,1)} %x_ref.1, f32[6656,128]{1,0:T(8,128)} %e_ref.1, f32[416,256]{1,0:T(8,128)} %v1_ref.1, f32[416,256]{1,0:T(8,128)} %v2_ref.1, f32[256,256]{1,0:T(8,128)} %t1_ref.1, f32[256,256]{1,0:T(8,128)} %t2_ref.1), custom_call_target="tpu_custom_call" | custom-call | tf_op jit(solution)/shard_map/pallas_call | solution.py:395
  74.3 1.5 %broadcast_multiply_fusion = f32[128,128]{1,0:T(8,128)} fusion(f32[128,128]{1,0:T(8,128)} %shard_map.73, f32[128]{0:T(128)S(1)} %rsqrt.3), kind=kLoop, calls=%fused_computation | loop fusion | flops 16384 | bytes 131584 | tf_op jit(solution)/shard_map/mul | solution.py:458

commit v6 on v4

--- a/solution.py
+++ b/solution.py
@@ -159,6 +159,8 @@
     for d in (1, 3):
         y_in[d].wait_recv()
         x_in[d] = x_stage(d)
+        if d == 3:
+            e_in += e_stage(1)
 
     def along_z(d):
         arrived(x_in[d][0])
@@ -168,8 +170,6 @@
 
     for d in (2, 1, 3, 0):
         along_z(d)
-        if d == 2:
-            e_in += e_stage(1)
 
     def forward(d):
         arrived(z_in[d])

time: 76.3 us -> 76.6 us (level)
  no operation moved by 1% of the time
where the time goes in v6:
time: 76.6 us; the launch traced here: 75.8 us
  Pallas kernels  73.7 us (96%)
  other arithmetic  1.48 us (2%)
    pallas_call x1, Pallas kernels, per_device(): pl.pallas_call(kernel, out_shape=jax.ShapeDtypeStruct((128, 128), F32), i...  73.7 us

profile of v6, /device:TPU:1, one launch (start us, length us, event | category | flops | bytes accessed | tf_op | source)
XLA Modules:
  0.0 75.8 jit_solution(15935043147658570065)
XLA Ops:
  0.0 0.7 rsqrt.3
  0.7 73.7 %shard_map.73 = f32[128,128]{1,0:T(8,128)} custom-call(bf16[8,53248]{1,0:T(8,128)(2,1)} %x_ref.1, f32[6656,128]{1,0:T(8,128)} %e_ref.1, f32[416,256]{1,0:T(8,128)} %v1_ref.1, f32[416,256]{1,0:T(8,128)} %v2_ref.1, f32[256,256]{1,0:T(8,128)} %t1_ref.1, f32[256,256]{1,0:T(8,128)} %t2_ref.1), custom_call_target="tpu_custom_call" | custom-call | tf_op jit(solution)/shard_map/pallas_call | solution.py:391
  74.3 1.5 %broadcast_multiply_fusion = f32[128,128]{1,0:T(8,128)} fusion(f32[128,128]{1,0:T(8,128)} %shard_map.73, f32[128]{0:T(128)S(1)} %rsqrt.3), kind=kLoop, calls=%fused_computation | loop fusion | flops 16384 | bytes 131584 | tf_op jit(solution)/shard_map/mul | solution.py:454
